TPU v7x, 512 devices: a whole 4x8x8 slice. The times are simulated.
512 devices in a mesh: vocab: 64 (over x, y, core), tok: 8 (over z).
Axes of the slice: x: 4, y: 8, z: 8, core: 2. Of those that a mesh axis runs over, the one named last changes fastest.
Arguments:
- hidden: bfloat16 [1024, 3584], P('tok'), may hold values from -320 to 320
- head: bfloat16 [3584, 98304], P('tok', 'vocab'), may hold values from -2 to 2
- teacher: bfloat16 [1024, 98304], P('tok', 'vocab'), may hold values from 0 to 1, as said below
- block_ids: int32 [8, 16], P('tok'), may hold values from -1 to 191, as said below
- counts: int32 [8], P('tok'), may hold values from 8 to 16
Outputs:
- lse: float32 [1024], P('tok')
- kl: float32 [1024], P('tok')
- grad_hidden: float32 [1024, 3584], P('tok', 'vocab')
- grad_head: bfloat16 [3584, 98304], P('tok', 'vocab')
Inputs may be any that keep to these rules, and one draw needn't show every extreme that they name: `block_ids`: row b lists counts[b] distinct teacher blocks (block k covers columns 512 * k to 512 * k + 511) in its first counts[b] entries; the rest of the row is -1. `teacher`: every entry is positive.
All inputs are finite; a program needn't handle non-finite values.
Results may differ from a plain program's by a relative error of at most 0.0055.
Values may be sent and summed in bfloat16 or wider, within the bound.
A program may use at most 64 MiB of HBM per device.

v0:
```python
import jax
import jax.numpy as jnp
from jax import lax
from jax.sharding import PartitionSpec as P

BLK = 512


loss_scale = 1024.0


def local_stats(logits, teacher, listed):
    teacher_f = teacher.astype(jnp.float32)
    kept = jnp.where(listed, teacher_f, 0.0)
    local_top = jnp.max(logits, axis=1)
    local_sum = jnp.sum(jnp.exp(logits - local_top[:, None]), axis=1)
    local_mass = jnp.sum(kept, axis=1)
    local_part = jnp.sum(jnp.where(listed, teacher_f * (jnp.log(teacher_f) - logits), 0.0), axis=1)
    return (kept, (local_top, local_sum, local_mass, local_part))


def finish_stats(logits, kept, global_top, total_sum, total_mass, total_part):
    lse = global_top + jnp.log(total_sum)
    kl = total_part / total_mass - jnp.log(total_mass) + lse
    student = jnp.exp(logits - lse[:, None])
    delta = (loss_scale * (student - kept / total_mass[:, None])).astype(jnp.bfloat16)
    return (lse, kl, delta)


def listed_columns(block_ids, counts, column_block, token_count):
    live_slot = jnp.arange(block_ids.shape[1], dtype=jnp.int32)[None, :] < counts[:, None]
    block_hit = jnp.any(
        (block_ids[:, :, None] == column_block[None, None, :]) & live_slot[:, :, None], axis=1
    )
    token_blocks = block_hit.shape[0]
    width = column_block.shape[0]
    return jnp.broadcast_to(
        block_hit[:, None, :], (token_blocks, token_count // token_blocks, width)
    ).reshape(token_count, width)


def per_device(hidden, head, teacher, block_ids, counts):
    token_count = hidden.shape[0]
    column_count = head.shape[1]
    full_head = lax.all_gather(head, "tok", axis=0, tiled=True)
    logits = jnp.dot(hidden, full_head, preferred_element_type=jnp.float32)
    first_column = lax.axis_index("vocab") * column_count
    column_block = (first_column + jnp.arange(column_count, dtype=jnp.int32)) // BLK
    listed = listed_columns(block_ids, counts, column_block, token_count)
    kept, stats_here = local_stats(logits, teacher, listed)
    local_top, local_sum, local_mass, local_part = stats_here
    global_top = lax.pmax(local_top, "vocab")
    scaled_sum = local_sum * jnp.exp(local_top - global_top)
    total_sum, total_mass, total_part = lax.psum((scaled_sum, local_mass, local_part), "vocab")
    lse, kl, delta = finish_stats(logits, kept, global_top, total_sum, total_mass, total_part)
    grad_hidden = lax.psum_scatter(
        lax.dot_general(
            full_head, delta, (((1,), (1,)), ((), ())), preferred_element_type=jnp.float32
        ),
        "vocab",
        scatter_dimension=0,
        tiled=True,
    ).T
    slices = lax.all_to_all(hidden, "tok", split_axis=1, concat_axis=0, tiled=True)
    grad_head = lax.dot_general(
        slices,
        lax.all_gather(delta, "tok", axis=0, tiled=True),
        (((0,), (0,)), ((), ())),
        preferred_element_type=jnp.float32,
    ).astype(jnp.bfloat16)
    return (lse, kl, grad_hidden, grad_head)


def solution(mesh):
    placed = (P("tok", None), P("tok", "vocab"), P("tok", "vocab"), P("tok", None), P("tok"))
    return jax.shard_map(
        per_device,
        mesh=mesh,
        in_specs=placed,
        out_specs=(P("tok"), P("tok"), P("tok", "vocab"), P("tok", "vocab")),
        check_vma=False,
    )
```

profile of v0, /device:TPU:1, one launch (start us, length us, event | category | flops | bytes accessed | tf_op | source)
XLA Modules:
  0.0 657.2 jit_solution(4507832720757288670)
XLA Ops:
  7.2 0.0 all-gather.3.cloned.1.call-start
  7.2 0.7 all-gather.3.cloned.1.call-update
  7.9 0.0 all-reduce.4.cloned.1.call-start
  8.6 0.8 and_reduce_fusion
  9.4 0.0 copy-start.2
  9.4 128.1 %all-gather.3.cloned.1.call-done = bf16[3584,1536]{1,0:T(8,128)(2,1)} async-done(((bf16[448,1536]{1,0:T(8,128)(2,1)}), bf16[3584,1536]{1,0:T(8,128)(2,1)}) %all-gather.3.cloned.1.call-update) | async-done | bytes 11010064 | tf_op jit(solution)/shard_map/all_gather | solution.py:45
  137.5 6.1 fusion.14
  143.6 124.3 %pmax.7 = f32[128]{0:T(128)S(1)} all-reduce(f32[128]{0:T(128)S(1)} %get-tuple-element.28), channel_id=1, replica_groups=mesh['vocab'=64,'tok'=8] {'vocab'}, use_global_device_ids=true, to_apply=%region_1.2 | all-reduce | flops 128 | bytes 1024 | tf_op jit(solution)/shard_map/pmax | solution.py:52
  267.8 0.0 copy-done.2
  267.8 0.5 fusion.9
  268.3 128.3 %all-reduce.1 = (f32[128]{0:T(128)S(1)}, f32[128]{0:T(128)S(1)}, f32[128]{0:T(128)S(1)}) all-reduce(f32[128]{0:T(128)S(1)} %exponential_multiply_fusion, f32[128]{0:T(128)S(1)} %get-tuple-element.22, f32[128]{0:T(128)S(1)} %get-tuple-element.20), channel_id=1, replica_groups=mesh['vocab'=64,'tok'=8] {'vocab'}, use_global_device_ids=true, to_apply=%region_3.4 | all-reduce | flops 384 | bytes 3072 | tf_op jit(solution)/shard_map/psum | solution.py:54
  396.6 0.5 subtract_add_fusion
  397.1 0.0 copy-start.3
  397.1 0.3 fusion.10
  397.4 0.0 copy-start.1
  397.4 0.0 copy-start
  397.4 9.1 %convolution_bitcast_fusion = f32[3584,128]{0,1:T(8,128)} fusion(bf16[128,1536]{1,0:T(8,128)(2,1)S(1)} %fusion.10, bf16[3584,1536]{1,0:T(8,128)(2,1)} %all-gather.3.cloned.1.call-done), kind=kOutput, calls=%fused_computation | convolution fusion | flops 1409286144 | bytes 13238272 | tf_op jit(solution)/shard_map/dot_general | solution.py:57
  406.6 0.0 copy-done.3
  406.6 0.0 copy-done.1
  406.6 0.0 all-reduce.4.cloned.1.call-update
  406.6 0.0 all-gather.5.cloned.1.call-start
  406.6 0.7 all-gather.5.cloned.1.call-update
  407.3 0.0 copy-done
  407.3 1.3 copy.16
  408.6 3.8 all-to-all-start
  412.4 1.3 dynamic-slice
  414.3 182.0 %all-reduce.4.cloned.1.call-done = f32[3584,128]{0,1:T(8,128)} async-done(((f32[3584,128]{0,1:T(8,128)}), f32[3584,128]{0,1:T(8,128)}) %all-reduce.4.cloned.1.call-update) | async-done | bytes 1835024
  596.3 1.0 dynamic-slice_bitcast_fusion
  597.3 0.7 copy.18
  598.0 0.0 all-to-all-done
  598.0 48.1 %all-gather.5.cloned.1.call-done = bf16[1024,1536]{1,0:T(8,128)(2,1)} async-done(((bf16[128,1536]{1,0:T(8,128)(2,1)}), bf16[1024,1536]{1,0:T(8,128)(2,1)}) %all-gather.5.cloned.1.call-update) | async-done | bytes 3145744 | tf_op jit(solution)/shard_map/all_gather | solution.py:67
  646.1 4.6 fusion
  (3 shorter events, 0.0 us)
Async XLA Ops:
  7.2 130.3 %all-gather.3.cloned.1.call-start = ((), (), s32[]{:S(2)}) async-start(), calls=%async_computation.1 | async-start | bytes 12386304 | tf_op jit(solution)/shard_map/all_gather | solution.py:45
  7.9 588.4 %all-reduce.4.cloned.1.call-start = ((), (), s32[]{:S(2)}) async-start(), calls=%async_computation.3 | async-start | bytes 3670016
  9.4 258.5 %copy-start.2 = (bf16[128,1536]{1,0:T(8,128)(2,1)S(1)}, bf16[128,1536]{1,0:T(8,128)(2,1)}, u32[]{:S(2)}) copy-start(bf16[128,1536]{1,0:T(8,128)(2,1)} %param.7) | copy-start | bytes 1179652
  397.1 9.5 %copy-start.3 = (f32[128]{0:T(128)}, f32[128]{0:T(128)S(1)}, u32[]{:S(2)}) copy-start(f32[128]{0:T(128)S(1)} %get-tuple-element.27) | copy-start | bytes 1540
  397.4 9.2 %copy-start.1 = (bf16[128,1536]{1,0:T(8,128)(2,1)}, bf16[128,1536]{1,0:T(8,128)(2,1)S(1)}, u32[]{:S(2)}) copy-start(bf16[128,1536]{1,0:T(8,128)(2,1)S(1)} %fusion.10) | copy-start | bytes 1179652
  397.4 9.9 %copy-start = (bf16[128,3584]{1,0:T(8,128)(2,1)S(1)}, bf16[128,3584]{1,0:T(8,128)(2,1)}, u32[]{:S(2)}) copy-start(bf16[128,3584]{1,0:T(8,128)(2,1)} %param.5) | copy-start | bytes 2752516
  406.6 239.5 %all-gather.5.cloned.1.call-start = ((), (), s32[]{:S(2)}) async-start(), calls=%async_computation.2 | async-start | bytes 3538944 | tf_op jit(solution)/shard_map/all_gather | solution.py:67
  408.6 189.4 %all-to-all-start = ((bf16[128,8,448]{0,2,1:T(8,128)(2,1)}), bf16[128,8,448]{0,2,1:T(8,128)(2,1)S(1)}, u32[]{:S(2)}, u32[]{:S(2)}) async-start(bf16[128,8,448]{0,2,1:T(8,128)(2,1)} %bitcast.4), calls=%async_computation | async-start | bytes 1835008 | tf_op jit(solution)/shard_map/all_to_all | solution.py:64
Sparse Core Ops, SparseCore 0:
  10.1 127.3 all-gather.2
  406.7 189.5 all-reduce.3
  598.4 47.6 all-gather.4
where the time goes:
time: 658 us; the launch traced here: 657 us
  waiting for transfers between devices  360 us (55%)
  blocking collectives  253 us (38%)
  matrix products  19.8 us (3%)
  between operations  15.1 us (2%)
    unnamed x4, waiting for transfers between devices  183 us
    psum x1, blocking collectives, per_device(): lax.psum((scaled_sum, local_mass, local_part), 'vocab')  128 us
    all_gather x1, waiting for transfers between devices, per_device(): full_head = lax.all_gather(head, 'tok', axis=0, tiled=True)  128 us
    pmax x1, blocking collectives, per_device(): global_top = lax.pmax(local_top, 'vocab')  124 us
    all_gather x1, waiting for transfers between devices, per_device(): lax.all_gather(delta, 'tok', axis=0, tiled=True)  48.1 us
  transfers between devices with their start and end apart: 4, of which 3 were waited for; matrix products, arithmetic and copies ran while one was open for 1% of the time, Pallas kernels for 0%

commit v1 on v0

v1 whole, which is shorter than its diff:
```python
import functools

import jax
import jax.numpy as jnp
from jax import lax
from jax.experimental import pallas as pl
from jax.experimental.pallas import tpu as pltpu
from jax.sharding import PartitionSpec as P

BLK = 512
RING_Y = 8

MESH = pl.DeviceIdType.MESH
loss_scale = 1024.0


def ring_hops(n, parts):
    if parts == 1:
        return [(n // 2, (n - 1) // 2)]
    return [(n // 2, (n - 1) // 2), ((n - 1) // 2, n // 2)]


def kernel_body(
    geo,
    hidden, head, teacher, ids, counts,
    ghead_out, ghid_out, stat_out,
    kept, hid, headt, teach, logits, stat, stat_in, delta, dg, hidt, res, gt, gc, gx, gy, gf, gsum, fin, fin_in,
    s_hz, r_hz, s_hp, r_hp, s_hd, s_hf, r_hd, s_te, r_te, s_st, r_st, s_dl, s_df, r_dl, s_ht, r_ht,
    s_gc, r_gc, s_gx, r_gx, s_gy, r_gy, s_go, r_go, s_fi, r_fi,
):
    X, Y, Z, blk = geo
    H = Z // 2
    tb, d = hidden.shape
    db, cb = head.shape
    cs = cb // H
    th = tb * H
    v = lax.axis_index("vocab")
    z = lax.axis_index("tok")
    c = lax.rem(v, 2)
    y = lax.rem(lax.div(v, 2), Y)
    x = lax.div(v, 2 * Y)
    zh, zl = lax.div(z, H), lax.rem(z, H)
    pc = 1 - c

    def dev(xx, yy, cc, zz):
        return {"vocab": (xx * Y + yy) * 2 + cc, "tok": zz}

    def rc(src, dst, ssem, rsem, device):
        return pltpu.make_async_remote_copy(
            src_ref=src, dst_ref=dst, send_sem=ssem, recv_sem=rsem, device_id=device, device_id_type=MESH
        )

    partner = dev(x, y, pc, z)
    order = sorted(range(1, Z), key=lambda o: -min(o, Z - o))

    pr, plan = tb // Y, d // X
    row0 = pl.multiple_of(y * pr, pr)
    lane0 = pl.multiple_of(x * plan, plan)
    piece = hidden.at[pl.ds(row0, pr), pl.ds(lane0, plan)]
    piece_to = hid.at[zl, pl.ds(row0, pr), pl.ds(lane0, plan)]

    def hz_copy(o):
        zd = lax.rem(z + o, Z)
        return zd, rc(piece, piece_to, s_hz.at[o], r_hz.at[zl], dev(x, y, zh, zd))

    for o in order:
        zd, copy = hz_copy(o)

        @pl.when(lax.div(zd, H) == c)
        def _():
            copy.start()

    @pl.when(zh == c)
    def _():
        pltpu.make_async_copy(piece, piece_to, r_hz.at[zl]).start()

    def hd_copy(o):
        zd = lax.rem(z + o, Z)
        cols = pl.ds(pl.multiple_of(lax.rem(zd, H) * cs, cs), cs)
        return zd, rc(head.at[:, cols], headt.at[z], s_hd.at[o], r_hd.at[z], dev(x, y, zh, zd))

    for o in order:
        zd, copy = hd_copy(o)

        @pl.when(lax.div(zd, H) == c)
        def _():
            copy.start()

    own_cols = pl.ds(pl.multiple_of(zl * cs, cs), cs)

    own_head = rc(head.at[:, own_cols], headt.at[z], s_hd.at[0], r_hd.at[z], partner)

    @pl.when(zh == c)
    def _():
        pltpu.make_async_copy(head.at[:, own_cols], headt.at[z], r_hd.at[z]).start()
        own_head.start()

    slots = ids.shape[1]
    for k in range(cb // blk):
        block = v * (cb // blk) + k
        hit = jnp.int32(0)
        for s in range(slots):
            hit = hit | jnp.where((ids[0, s] == block) & (s < counts[0]), 1, 0)
        part = teacher[:, k * blk : (k + 1) * blk]
        keep = jnp.full(part.shape, hit, jnp.int32) > 0
        kept[:, k * blk : (k + 1) * blk] = jnp.where(keep, part.astype(jnp.float32), 0.0).astype(jnp.bfloat16)

    def te_copy(o):
        zd = lax.rem(z + o, Z)
        cols = pl.ds(pl.multiple_of(lax.rem(zd, H) * cs, cs), cs)
        return zd, rc(kept.at[:, cols], teach.at[zl], s_te.at[o], r_te.at[zl], dev(x, y, zh, zd))

    for o in order:
        zd, copy = te_copy(o)

        @pl.when(lax.div(zd, H) == c)
        def _():
            copy.start()

    @pl.when(zh == c)
    def _():
        pltpu.make_async_copy(kept.at[:, own_cols], teach.at[zl], r_te.at[zl]).start()

    for k in range(H):
        pltpu.make_async_copy(piece, hid.at[k, pl.ds(row0, pr), pl.ds(lane0, plan)], r_hz.at[k]).wait()

    parts = [(0, H)] if H == 1 else [(0, H // 2), (H // 2, H // 2)]

    def ring(n, me, slot, neighbour, ssem, rsem):
        if n == 1:
            return
        hops = ring_hops(n, len(parts))

        def copy(pi, direction, s):
            index = lax.rem(me - (s - 1) + n, n) if direction == 0 else lax.rem(me + (s - 1), n)
            to = lax.rem(me + 1, n) if direction == 0 else lax.rem(me + n - 1, n)
            view = slot(index, parts[pi])
            return rc(view, view, ssem.at[pi, direction, s - 1], rsem.at[pi, direction, s - 1], neighbour(to))

        def arrived(pi, direction, s):
            index = lax.rem(me - s + n, n) if direction == 0 else lax.rem(me + s, n)
            view = slot(index, parts[pi])
            pltpu.make_async_copy(view, view, rsem.at[pi, direction, s - 1]).wait()

        for s in range(1, n // 2 + 1):
            for pi in range(len(parts)):
                for direction in range(2):
                    if s <= hops[pi][direction]:
                        if s > 1:
                            arrived(pi, direction, s - 1)
                        copy(pi, direction, s).start()
        for pi in range(len(parts)):
            for direction in range(2):
                if hops[pi][direction] > 0:
                    arrived(pi, direction, hops[pi][direction])
        for s in range(1, n // 2 + 1):
            for pi in range(len(parts)):
                for direction in range(2):
                    if s <= hops[pi][direction]:
                        copy(pi, direction, s).wait_send()

    def rows_at(i):
        return pl.ds(pl.multiple_of(i * pr, pr), pr)

    def lanes_at(i):
        return pl.ds(pl.multiple_of(i * plan, plan), plan)

    def to_x(i):
        return dev(i, y, c, z)

    def to_y(i):
        return dev(x, i, c, z)

    @pl.when(c == 0)
    def _():
        ring(X, x, lambda i, p: hid.at[pl.ds(*p), rows_at(y), lanes_at(i)], to_x, s_hp.at[0], r_hp.at[0])
        ring(Y, y, lambda i, p: hid.at[pl.ds(*p), rows_at(i), :], to_y, s_hp.at[1], r_hp.at[1])

    @pl.when(c == 1)
    def _():
        ring(Y, y, lambda i, p: hid.at[pl.ds(*p), rows_at(i), lanes_at(x)], to_y, s_hp.at[0], r_hp.at[0])
        ring(X, x, lambda i, p: hid.at[pl.ds(*p), :, lanes_at(i)], to_x, s_hp.at[1], r_hp.at[1])

    def hf_copy(zs):
        return rc(headt.at[zs], headt.at[zs], s_hf.at[lax.rem(zs, H)], r_hd.at[zs], partner)

    def head_arrived(zs):
        pltpu.make_async_copy(headt.at[zs], headt.at[zs], r_hd.at[zs]).wait()

    for o in reversed(order):
        zs = lax.rem(z + o, Z)

        @pl.when(lax.div(zs, H) == c)
        def _():
            head_arrived(zs)
            hf_copy(zs).start()

    win = hidt.shape[1]
    win0 = lax.div(z * db, 128) * 128
    off = z * db - win0
    for k in range(H):
        block = hid[k, :, pl.ds(pl.multiple_of(win0, 128), win)]
        hidt[c, :, k * tb : (k + 1) * tb] = block.T
    ht_copy = rc(hidt.at[c], hidt.at[c], s_ht, r_ht, partner)
    ht_copy.start()

    @pl.when(zh == c)
    def _():
        head_arrived(z)

    for o in reversed(order):
        zs = lax.rem(z + o, Z)

        @pl.when(lax.div(zs, H) != c)
        def _():
            head_arrived(zs)

    @pl.when(zh != c)
    def _():
        head_arrived(z)

    logits[...] = jnp.zeros_like(logits)
    kd = 2 * db

    @pl.loop(0, H)
    def _(p):
        lhs = hid[:, :, pl.ds(pl.multiple_of(p * kd, kd), kd)].reshape(th, kd)
        rhs = headt[pl.ds(2 * p, 2)].reshape(kd, cs)
        logits[...] += jnp.dot(lhs, rhs, preferred_element_type=jnp.float32)

    for k in range(H):
        pltpu.make_async_copy(teach.at[k], teach.at[k], r_te.at[k]).wait()

    lane = lax.broadcasted_iota(jnp.int32, (tb, 128), 1)

    for k in range(H):
        lk = logits[k * tb : (k + 1) * tb, :]
        tk = teach[k].astype(jnp.float32)
        top = jnp.max(lk, axis=1, keepdims=True)
        total = jnp.sum(jnp.exp(lk - top), axis=1, keepdims=True)
        mass = jnp.sum(tk, axis=1, keepdims=True)
        live = tk > 0.0
        term = jnp.where(live, tk * (jnp.log(jnp.where(live, tk, 1.0)) - lk), 0.0)
        weighted = jnp.sum(term, axis=1, keepdims=True)
        table = jnp.where(
            lane == 0, top, jnp.where(lane == 1, total, jnp.where(lane == 2, mass, weighted))
        ).T
        for q in range(4):
            stat[q * H + k : q * H + k + 1, :] = table[q : q + 1, :]

    def combine(blocks):
        tops = [b[0:H] for b in blocks]
        top = functools.reduce(jnp.maximum, tops)
        total = functools.reduce(jnp.add, [b[H : 2 * H] * jnp.exp(t - top) for b, t in zip(blocks, tops)])
        rest = functools.reduce(jnp.add, [b[2 * H :] for b in blocks])
        return top, total, rest

    def exchange(stage, n, me, to):
        if n == 1:
            return
        others = sorted(range(1, n), key=lambda o: -min(o, n - o))

        def copy(o):
            return rc(
                stat.at[...],
                stat_in.at[stage, n - o],
                s_st.at[stage, o],
                r_st.at[stage, n - o],
                to(lax.rem(me + o, n)),
            )

        for o in others:
            copy(o).start()
        for o in reversed(others):
            copy(o).wait_send()
        blocks = [stat[...]]
        for o in range(1, n):
            pltpu.make_async_copy(stat.at[...], stat_in.at[stage, o], r_st.at[stage, o]).wait()
        for o in range(1, n):
            blocks.append(stat_in[stage, o])
        top, total, rest = combine(blocks)
        stat[0:H, :] = top
        stat[H : 2 * H, :] = total
        stat[2 * H : 4 * H, :] = rest

    exchange(0, X, x, to_x)
    exchange(1, Y, y, to_y)
    exchange(2, Z, z, lambda i: dev(x, y, c, i))

    final = stat[...]
    lse = final[0:H] + jnp.log(final[H : 2 * H])
    mass = final[2 * H : 3 * H]
    kl = final[3 * H : 4 * H] / mass - jnp.log(mass) + lse
    scale = loss_scale / mass
    rows = jnp.concatenate([lse, scale, jnp.zeros((128 - 2 * H, 128), jnp.float32)], axis=0).T

    for k in range(H):
        lk = logits[k * tb : (k + 1) * tb, :]
        tk = teach[k].astype(jnp.float32)
        student = jnp.exp(lk - rows[:, k : k + 1])
        delta[k * tb : (k + 1) * tb, :] = (loss_scale * student - tk * rows[:, H + k : H + k + 1]).astype(
            jnp.bfloat16
        )

    hops = ring_hops(Z, 2)

    def dl_copy(direction):
        to = lax.rem(z + 1, Z) if direction == 0 else lax.rem(z + Z - 1, Z)
        return rc(delta.at[...], dg.at[zl, c], s_dl.at[direction], r_dl.at[zl, c], dev(x, y, zh, to))

    dl_copy(0).start()
    if hops[1][1] > 0 and hops[0][1] > 0:
        dl_copy(1).start()
    else:

        @pl.when(c == 1)
        def _():
            dl_copy(1).start()

    dl_local = rc(delta.at[...], dg.at[zl, c], s_dl.at[2], r_dl.at[zl, c], partner)

    @pl.when(zh != c)
    def _():
        dl_local.start()

    @pl.when(zh == c)
    def _():
        pltpu.make_async_copy(delta.at[...], dg.at[zl, c], r_dl.at[zl, c]).start()

    pick = lax.broadcasted_iota(jnp.int32, (H, 128), 0) == zl
    fin[0:1, :] = jnp.sum(jnp.where(pick, lse, 0.0), axis=0, keepdims=True)
    fin[1:2, :] = jnp.sum(jnp.where(pick, kl, 0.0), axis=0, keepdims=True)
    fi_copy = rc(fin.at[...], fin_in.at[...], s_fi, r_fi, partner)
    fi_copy.start()

    gt[...] = jnp.zeros_like(gt)
    pltpu.make_async_copy(hidt.at[pc], hidt.at[pc], r_ht).wait()

    def consume(kk):
        cols = pl.ds(pl.multiple_of(kk * cs, cs), cs)
        for h in range(2):
            gt[h] += lax.dot_general(
                head[:, cols], dg[kk, h], (((1,), (1,)), ((), ())), preferred_element_type=jnp.float32
            )
        res[...] = jnp.dot(hidt[0], dg[kk, 0], preferred_element_type=jnp.float32) + jnp.dot(
            hidt[1], dg[kk, 1], preferred_element_type=jnp.float32
        )
        ghead_out[:, cols] = res[pl.ds(pl.multiple_of(off, 64), db), :].astype(jnp.bfloat16)

    def dl_arrived(kk, part):
        pltpu.make_async_copy(dg.at[kk, part], dg.at[kk, part], r_dl.at[kk, part]).wait()

    def df_copy(kk, part, direction):
        to = lax.rem(z + 1, Z) if direction == 0 else lax.rem(z + Z - 1, Z)
        view = dg.at[kk, part]
        return rc(view, view, s_df.at[kk, part], r_dl.at[kk, part], dev(x, y, c, to))

    for s in range(1, Z // 2 + 1):
        for part in range(2):
            for direction in range(2):
                if s <= hops[part][direction]:
                    zs = lax.rem(z - s + Z, Z) if direction == 0 else lax.rem(z + s, Z)
                    kk = lax.rem(zs, H)

                    @pl.when(lax.div(zs, H) == c)
                    def _():
                        dl_arrived(kk, part)
                        if s < hops[part][direction]:
                            df_copy(kk, part, direction).start()

    @pl.when(zh == c)
    def _():
        dl_arrived(zl, 0)
        dl_arrived(zl, 1)

    @pl.loop(0, H)
    def _(kk):
        consume(kk)

    gc_copy = rc(gt.at[pc], gc.at[...], s_gc, r_gc, partner)
    gc_copy.start()
    gc_copy.wait()
    gsum[...] = gt[c] + gc[...]

    def gx_copy(o):
        xd = lax.rem(x + o, X)
        lanes = pl.ds(pl.multiple_of(xd * tb, tb), tb)
        return rc(gsum.at[:, lanes], gx.at[X - o], s_gx.at[o], r_gx.at[X - o], to_x(xd))

    for o in range(1, X):
        gx_copy(o).start()
    acc = gsum[:, pl.ds(pl.multiple_of(x * tb, tb), tb)]
    for o in range(1, X):
        gx_copy(o).wait_send()
        pltpu.make_async_copy(gx.at[o], gx.at[o], r_gx.at[o]).wait()
    for o in range(1, X):
        acc = acc + gx[o]
    gx[0] = acc

    sub = db // Y

    def gy_copy(o):
        yd = lax.rem(y + o, Y)
        return rc(
            gx.at[0, pl.ds(pl.multiple_of(yd * sub, sub), sub), :],
            gy.at[Y - o],
            s_gy.at[o],
            r_gy.at[Y - o],
            to_y(yd),
        )

    for o in range(1, Y):
        gy_copy(o).start()
    acc = gx[0, pl.ds(pl.multiple_of(y * sub, sub), sub), :]
    for o in range(1, Y):
        gy_copy(o).wait_send()
        pltpu.make_async_copy(gy.at[o], gy.at[o], r_gy.at[o]).wait()
    for o in range(1, Y):
        acc = acc + gy[o]
    gf[0] = acc

    vt, zt = z * Y + y, c * X + x
    at_home = (vt == v) & (zt == z)
    go_copy = rc(gf.at[0], gf.at[1], s_go, r_go, {"vocab": vt, "tok": zt})
    go_local = pltpu.make_async_copy(gf.at[0], gf.at[1], r_go)

    @pl.when(at_home)
    def _():
        go_local.start()

    @pl.when(jnp.logical_not(at_home))
    def _():
        go_copy.start()

    pltpu.make_async_copy(fin_in.at[...], fin_in.at[...], r_fi).wait()
    mine = jnp.full(fin.shape, jnp.where(zh == c, 1, 0), jnp.int32) > 0
    stat_out[...] = jnp.where(mine, fin[...], fin_in[...])

    for o in order:
        zd, copy = hz_copy(o)

        @pl.when(lax.div(zd, H) == c)
        def _():
            copy.wait_send()

        zd, copy = hd_copy(o)

        @pl.when(lax.div(zd, H) == c)
        def _():
            copy.wait_send()

        zd, copy = te_copy(o)

        @pl.when(lax.div(zd, H) == c)
        def _():
            copy.wait_send()

        zs = lax.rem(z + o, Z)

        @pl.when(lax.div(zs, H) == c)
        def _():
            hf_copy(zs).wait_send()

    @pl.when(zh == c)
    def _():
        own_head.wait_send()

    ht_copy.wait_send()
    dl_copy(0).wait_send()
    if hops[1][1] > 0 and hops[0][1] > 0:
        dl_copy(1).wait_send()
    else:

        @pl.when(c == 1)
        def _():
            dl_copy(1).wait_send()

    @pl.when(zh != c)
    def _():
        dl_local.wait_send()

    fi_copy.wait_send()
    for s in range(1, Z // 2 + 1):
        for part in range(2):
            for direction in range(2):
                if s < hops[part][direction]:
                    zs = lax.rem(z - s + Z, Z) if direction == 0 else lax.rem(z + s, Z)

                    @pl.when(lax.div(zs, H) == c)
                    def _():
                        df_copy(lax.rem(zs, H), part, direction).wait_send()

    @pl.when(jnp.logical_not(at_home))
    def _():
        go_copy.wait_send()

    go_local.wait()
    ghid_out[...] = gf[1]


def per_device(geo, hidden, head, teacher, block_ids, counts):
    X, Y, Z, blk = geo
    H = Z // 2
    tb, d = hidden.shape
    db, cb = head.shape
    cs, th = cb // H, tb * H
    win = -(-db // 128) * 128
    sub = db // Y
    f32, bf16 = jnp.float32, jnp.bfloat16
    dma = pltpu.SemaphoreType.DMA
    half = max(X, Y) // 2
    scratch = [
        pltpu.VMEM((tb, cb), bf16),
        pltpu.VMEM((H, tb, d), bf16),
        pltpu.VMEM((Z, db, cs), bf16),
        pltpu.VMEM((H, tb, cs), bf16),
        pltpu.VMEM((th, cs), f32),
        pltpu.VMEM((4 * H, 128), f32),
        pltpu.VMEM((3, max(X, Y, Z), 4 * H, 128), f32),
        pltpu.VMEM((th, cs), bf16),
        pltpu.VMEM((H, 2, th, cs), bf16),
        pltpu.VMEM((2, win, th), bf16),
        pltpu.VMEM((win, cs), f32),
        pltpu.VMEM((2, db, th), f32),
        pltpu.VMEM((db, th), f32),
        pltpu.VMEM((X, db, tb), f32),
        pltpu.VMEM((Y, sub, tb), f32),
        pltpu.VMEM((2, sub, tb), f32),
        pltpu.VMEM((db, th), f32),
        pltpu.VMEM((8, 128), f32),
        pltpu.VMEM((8, 128), f32),
        dma((Z,)), dma((H,)),
        dma((2, 2, 2, half)), dma((2, 2, 2, half)),
        dma((Z,)), dma((H,)), dma((Z,)),
        dma((Z,)), dma((H,)),
        dma((3, max(X, Y, Z))), dma((3, max(X, Y, Z))),
        dma((3,)), dma((H, 2)), dma((H, 2)),
        dma, dma,
        dma, dma,
        dma((X,)), dma((X,)),
        dma((Y,)), dma((Y,)),
        dma, dma,
        dma, dma,
    ]
    vm = pl.BlockSpec(memory_space=pltpu.VMEM)
    sm = pl.BlockSpec(memory_space=pltpu.SMEM)
    ghead, ghid, stats = pl.pallas_call(
        functools.partial(kernel_body, geo),
        out_shape=(
            jax.ShapeDtypeStruct((db, cb), bf16),
            jax.ShapeDtypeStruct((sub, tb), f32),
            jax.ShapeDtypeStruct((8, 128), f32),
        ),
        in_specs=[vm, vm, vm, sm, sm],
        out_specs=(vm, vm, vm),
        scratch_shapes=scratch,
        compiler_params=pltpu.CompilerParams(has_side_effects=True, vmem_limit_bytes=60 * 2**20),
    )(hidden, head, teacher, block_ids, counts)
    return stats[0], stats[1], ghid.T, ghead


def solution(mesh, ring_y=RING_Y, blk=BLK):
    vocab, tok = mesh.shape["vocab"], mesh.shape["tok"]
    geo = (vocab // (2 * ring_y), ring_y, tok, blk)
    placed = (P("tok", None), P("tok", "vocab"), P("tok", "vocab"), P("tok", None), P("tok"))
    return jax.shard_map(
        functools.partial(per_device, geo),
        mesh=mesh,
        in_specs=placed,
        out_specs=(P("tok"), P("tok"), P("tok", "vocab"), P("tok", "vocab")),
        check_vma=False,
    )
```

time: 658 us -> 169 us (0.26)
  the two profiles are of different devices: /device:TPU:1 before, /device:TPU:21 now
where the time goes in v1:
time: 169 us; the launch traced here: 168 us
  Pallas kernels  162 us (96%)
  local copies, waits for them, and re-layouts  5.13 us (3%)
    pallas_call x1, Pallas kernels, per_device(): pl.pallas_call(functools.partial(kernel_body, geo), out_shape=(jax.ShapeD...  162 us
    unnamed x2, local copies, waits for them, and re-layouts  3.86 us

profile of v1, /device:TPU:21, one launch (start us, length us, event | category | flops | bytes accessed | tf_op | source)
XLA Modules:
  0.0 168.4 jit_solution(13428665507947358148)
XLA Ops:
  1.3 162.0 %shard_map.84 = (bf16[448,1536]{1,0:T(8,128)(2,1)}, f32[56,128]{1,0:T(8,128)}, f32[8,128]{1,0:T(8,128)}) custom-call(bf16[128,3584]{1,0:T(8,128)(2,1)} %hidden.1, bf16[448,1536]{1,0:T(8,128)(2,1)} %head.1, bf16[128,1536]{1,0:T(8,128)(2,1)} %teacher.1, s32[1,16]{1,0:T(1,128)} %ids.1, s32[1]{0:T(128)S(6)} %copy.11.counts), custom_call_target="tpu_custom_call" | custom-call | tf_op jit(solution)/shard_map/pallas_call | solution.py:547
  163.3 1.3 slice_bitcast_fusion
  164.6 1.4 copy.12
  165.9 2.5 %copy.13 = bf16[448,1536]{1,0:T(8,128)(2,1)} copy(bf16[448,1536]{1,0:T(8,128)(2,1)} %get-tuple-element.19) | data formatting | bytes 2752512

commit v2 on v1

v2 whole, which is shorter than its diff:
```python
import functools

import jax
import jax.numpy as jnp
from jax import lax
from jax.experimental import pallas as pl
from jax.experimental.pallas import tpu as pltpu
from jax.sharding import PartitionSpec as P

BLK = 512
RING_Y = 8

MESH = pl.DeviceIdType.MESH
loss_scale = 1024.0


def ring_hops(n, parts):
    if parts == 1:
        return [(n // 2, (n - 1) // 2)]
    return [(n // 2, (n - 1) // 2), ((n - 1) // 2, n // 2)]


def kernel_body(
    geo,
    hidden, head_in, teacher_in, ids, counts,
    ghead_out, ghid_out, stat_out,
    head, teacher, kept, hid, headt, teach, logits, masses, mass_in, terms, term_in, stat, stat_in, delta, dg, hidt, res, ghead, gt, gc, gx, gy, gf, gsum, fin, fin_in,
    s_in, s_gh, s_hz, r_hz, s_ga, r_ga, r_gb, s_hd, s_hf, r_hd, s_te, r_te, s_ms, r_ms, s_tm, r_tm, s_tz, s_st, r_st, s_dl, s_df, r_dl, s_ht, r_ht,
    s_gc, r_gc, s_gx, r_gx, s_gy, r_gy, s_go, r_go, s_fi, r_fi,
):
    X, Y, Z, blk = geo
    H = Z // 2
    tb, d = hidden.shape
    db, cb = head_in.shape
    cs = cb // H
    th = tb * H
    v = lax.axis_index("vocab")
    z = lax.axis_index("tok")
    c = lax.rem(v, 2)
    y = lax.rem(lax.div(v, 2), Y)
    x = lax.div(v, 2 * Y)
    zh, zl = lax.div(z, H), lax.rem(z, H)
    pc = 1 - c

    def dev(xx, yy, cc, zz):
        return {"vocab": (xx * Y + yy) * 2 + cc, "tok": zz}

    def rc(src, dst, ssem, rsem, device):
        return pltpu.make_async_remote_copy(
            src_ref=src, dst_ref=dst, send_sem=ssem, recv_sem=rsem, device_id=device, device_id_type=MESH
        )

    partner = dev(x, y, pc, z)

    def rows_of(yy, zz):
        return lax.rem(yy + Y // 4 + (Y // 2) * lax.rem(zz, 2), Y)

    def tokens_of(xx, cc, zz):
        same = lax.rem(cc + lax.div(zz, H) + 1, 2)
        return lax.rem(lax.rem(zz, H) + xx + X - lax.div(zz, 2) + (H // 2) * same, H)

    vt, zt = z * Y + rows_of(y, z), c * H + tokens_of(x, c, z)
    at_home = (vt == v) & (zt == z)
    zs_home, cs_home = lax.div(v, Y), zh
    same_home = lax.rem(cs_home + lax.div(zs_home, H) + 1, 2)
    ys_home = lax.rem(lax.rem(v, Y) + 2 * Y - Y // 4 - (Y // 2) * lax.rem(zs_home, 2), Y)
    xs_home = lax.rem(zl + 2 * H - lax.rem(zs_home, H) - (H // 2) * same_home + lax.div(zs_home, 2), X)
    vs = (xs_home * Y + ys_home) * 2 + cs_home

    barrier = pltpu.get_barrier_semaphore()

    def greet(device):
        pl.semaphore_signal(barrier, inc=1, device_id=device, device_id_type=MESH)

    greet(partner)
    for o in range(1, Z):
        for cc in range(2):
            greet(dev(x, y, cc, lax.rem(z + o, Z)))
    for o in range(1, X):
        greet(dev(lax.rem(x + o, X), y, c, z))
    for o in range(1, Y):
        greet(dev(x, lax.rem(y + o, Y), c, z))

    @pl.when(jnp.logical_not(at_home))
    def _():
        greet({"vocab": vt, "tok": zt})
        greet({"vocab": vs, "tok": zs_home})

    head_copy = pltpu.make_async_copy(head_in, head, s_in.at[0])
    teacher_copy = pltpu.make_async_copy(teacher_in, teacher, s_in.at[1])
    teacher_copy.start()
    head_copy.start()

    near = 1 + 2 * (Z - 1) + (X - 1) + (Y - 1)
    pl.semaphore_wait(barrier, jnp.where(at_home, near, near + 2))

    order = sorted(range(1, Z), key=lambda o: min(o, Z - o))

    pr, plan = tb // Y, d // X
    row0 = pl.multiple_of(y * pr, pr)
    lane0 = pl.multiple_of(x * plan, plan)
    piece = hidden.at[pl.ds(row0, pr), pl.ds(lane0, plan)]
    piece_to = hid.at[zl, pl.ds(row0, pr), pl.ds(lane0, plan)]

    def hz_copy(o):
        zd = lax.rem(z + o, Z)
        return zd, rc(piece, piece_to, s_hz.at[o], r_hz.at[zl], dev(x, y, zh, zd))

    for o in order:
        zd, copy = hz_copy(o)

        @pl.when(lax.div(zd, H) == c)
        def _():
            copy.start()

    @pl.when(zh == c)
    def _():
        pltpu.make_async_copy(piece, piece_to, r_hz.at[zl]).start()

    def hd_copy(o):
        zd = lax.rem(z + o, Z)
        cols = pl.ds(pl.multiple_of(lax.rem(zd, H) * cs, cs), cs)
        return zd, rc(head_in.at[:, cols], headt.at[z], s_hd.at[o], r_hd.at[z], dev(x, y, zh, zd))

    for o in order:
        zd, copy = hd_copy(o)

        @pl.when(lax.div(zd, H) == c)
        def _():
            copy.start()

    own_cols = pl.ds(pl.multiple_of(zl * cs, cs), cs)

    own_head = rc(head_in.at[:, own_cols], headt.at[z], s_hd.at[0], r_hd.at[z], partner)

    @pl.when(zh == c)
    def _():
        pltpu.make_async_copy(head_in.at[:, own_cols], headt.at[z], r_hd.at[z]).start()
        own_head.start()

    slots = ids.shape[1]
    teacher_copy.wait()
    local_mass = jnp.zeros((tb, 1), jnp.float32)
    for k in range(cb // blk):
        block = v * (cb // blk) + k
        hit = jnp.int32(0)
        for s in range(slots):
            hit = hit | jnp.where((ids[0, s] == block) & (s < counts[0]), 1, 0)
        part = teacher[:, k * blk : (k + 1) * blk]
        keep = jnp.full(part.shape, hit, jnp.int32) > 0
        part = jnp.where(keep, part.astype(jnp.float32), 0.0)
        kept[:, k * blk : (k + 1) * blk] = part.astype(jnp.bfloat16)
        local_mass = local_mass + jnp.sum(part, axis=1, keepdims=True)

    def te_copy(o):
        zd = lax.rem(z + o, Z)
        cols = pl.ds(pl.multiple_of(lax.rem(zd, H) * cs, cs), cs)
        return zd, rc(kept.at[:, cols], teach.at[zl], s_te.at[o], r_te.at[zl], dev(x, y, zh, zd))

    for o in order:
        zd, copy = te_copy(o)

        @pl.when(lax.div(zd, H) == c)
        def _():
            copy.start()

    @pl.when(zh == c)
    def _():
        pltpu.make_async_copy(kept.at[:, own_cols], teach.at[zl], r_te.at[zl]).start()

    masses[...] = jnp.broadcast_to(local_mass, (tb, 128)).T[0:8, :]

    def share(buffer, inbox, ssem, rsem, n, me, to):
        def start():
            for o in range(1, n):
                rc(buffer, inbox.at[n - o], ssem, rsem, to(lax.rem(me + o, n))).start()

        def arrive():
            if n > 1:
                all_in = inbox.at[pl.ds(1, n - 1)]
                pltpu.make_async_copy(all_in, all_in, ssem).wait()
                pltpu.make_async_copy(all_in, all_in, rsem).wait()

        return start, arrive

    def to_x(i):
        return dev(i, y, c, z)

    def to_y(i):
        return dev(x, i, c, z)

    def summed(buffer, inbox, n):
        total = buffer[...]
        for o in range(1, n):
            total = total + inbox[o]
        buffer[...] = total

    mass_c = rc(masses.at[...], mass_in.at[0, 0], s_ms.at[0], r_ms.at[0], partner)
    mass_x = share(masses.at[...], mass_in.at[1], s_ms.at[1], r_ms.at[1], X, x, to_x)
    mass_y = share(masses.at[...], mass_in.at[2], s_ms.at[2], r_ms.at[2], Y, y, to_y)
    mass_c.start()
    mass_c.wait()
    masses[...] = masses[...] + mass_in[0, 0]
    mass_x[0]()

    for k in range(H):
        pltpu.make_async_copy(piece, hid.at[k, pl.ds(row0, pr), pl.ds(lane0, plan)], r_hz.at[k]).wait()

    def gather(g, first, second, block):
        (n1, me1, to1), (n2, me2, to2) = first, second
        hops1 = ring_hops(n1, 1)[0]

        def along(n, me, direction, s, to):
            source = lax.rem(me - (s - 1) + n, n) if direction == 0 else lax.rem(me + (s - 1), n)
            target = lax.rem(me + 1, n) if direction == 0 else lax.rem(me + n - 1, n)
            return source, to(target)

        def came(n, me, direction, s):
            return lax.rem(me - s + n, n) if direction == 0 else lax.rem(me + s, n)

        def send1(direction, s):
            source, device = along(n1, me1, direction, s, to1)
            view = block(source, me2)
            rc(view, view, s_ga.at[g, 0], r_ga.at[g, direction, s - 1], device).start()

        def wait1(direction, s):
            view = block(came(n1, me1, direction, s), me2)
            pltpu.make_async_copy(view, view, r_ga.at[g, direction, s - 1]).wait()

        def hops2(q):
            right, left = ring_hops(n2, 1)[0]
            return (right, left) if q % 2 == 0 else (left, right)

        def send2(q, direction, s):
            source, device = along(n2, me2, direction, s, to2)
            view = block(lax.rem(me1 + q, n1), source)
            rc(view, view, s_ga.at[g, 1], r_gb.at[g, (2 * q + direction) * (n2 // 2) + s - 1], device).start()

        progress = {}

        def begin2(q):
            progress[q] = 1
            for direction in range(2):
                if hops2(q)[direction] >= 1:
                    send2(q, direction, 1)

        def advance2(q):
            s = progress[q]
            progress[q] += 1
            for direction in range(2):
                if s <= hops2(q)[direction]:
                    view = block(lax.rem(me1 + q, n1), came(n2, me2, direction, s))
                    pltpu.make_async_copy(view, view, r_gb.at[g, (2 * q + direction) * (n2 // 2) + s - 1]).wait()
                    if s < hops2(q)[direction]:
                        send2(q, direction, s + 1)

        for direction in range(2):
            if hops1[direction] >= 1:
                send1(direction, 1)
        begin2(0)
        yield
        for s in range(1, n1 // 2 + 1):
            earlier = list(progress)
            for direction in range(2):
                if s <= hops1[direction]:
                    wait1(direction, s)
                    if s < hops1[direction]:
                        send1(direction, s + 1)
                    begin2(n1 - s if direction == 0 else s)
            yield
            for q in earlier:
                if progress[q] <= n2 // 2:
                    advance2(q)
                    yield
        while any(at <= n2 // 2 for at in progress.values()):
            for q in list(progress):
                if progress[q] <= n2 // 2:
                    advance2(q)
                    yield
    def rows_at(i):
        return pl.ds(pl.multiple_of(i * pr, pr), pr)

    def lanes_at(i):
        return pl.ds(pl.multiple_of(i * plan, plan), plan)

    def hf_copy(zs):
        return rc(headt.at[zs], headt.at[zs], s_hf.at[lax.rem(zs, H)], r_hd.at[zs], partner)

    def head_arrived(zs):
        pltpu.make_async_copy(headt.at[zs], headt.at[zs], r_hd.at[zs]).wait()

    def head_onward(o):
        zs = lax.rem(z + o, Z)

        @pl.when(lax.div(zs, H) == c)
        def _():
            head_arrived(zs)
            hf_copy(zs).start()

    early = Z // 4
    split = H if H == 1 else H // 2
    x_first = gather(
        0, (X, x, to_x), (Y, y, to_y), lambda i, j: hid.at[pl.ds(0, split), rows_at(j), lanes_at(i)]
    )
    y_first = gather(
        1, (Y, y, to_y), (X, x, to_x), lambda i, j: hid.at[pl.ds(split, H - split), rows_at(i), lanes_at(j)]
    )
    todo = [x_first] if split == H else [x_first, y_first]
    turn = 0
    while todo:
        todo = [walk for walk in todo if next(walk, todo) is not todo]
        turn += 1
        if turn == 3:
            mass_x[1]()
            summed(masses, mass_in.at[1], X)
            mass_y[0]()
        if turn == 10 and early >= 1:
            head_onward(1)
            head_onward(Z - 1)
    if turn < 3:
        mass_x[1]()
        summed(masses, mass_in.at[1], X)
        mass_y[0]()
    if turn < 10 and early >= 1:
        head_onward(1)
        head_onward(Z - 1)
    for o in range(2, early + 1):
        head_onward(o)
        head_onward(Z - o)

    mass_y[1]()
    summed(masses, mass_in.at[2], Y)

    win = hidt.shape[1]
    win0 = lax.div(z * db, 128) * 128
    off = z * db - win0
    for k in range(H):
        block = hid[k, :, pl.ds(pl.multiple_of(win0, 128), win)]
        hidt[c, :, k * tb : (k + 1) * tb] = block.T
    ht_copy = rc(hidt.at[c], hidt.at[c], s_ht, r_ht, partner)
    ht_copy.start()

    logits[...] = jnp.zeros_like(logits)
    kd = 2 * db
    for step in [0] + [q * sign for q in range(1, H // 2 + 1) for sign in (1, -1)][: H - 1]:
        p = lax.rem(lax.div(z, 2) + step + H, H)
        for zs in (2 * p, 2 * p + 1):

            away = lax.rem(zs - z + Z, Z)
            passed = (away != 0) & ((away <= early) | (away >= Z - early)) & (lax.div(zs, H) == c)
            onward = (away > early) & (away < Z - early) & (lax.div(zs, H) == c)

            @pl.when(jnp.logical_not(passed))
            def _():
                head_arrived(zs)

            @pl.when(onward)
            def _():
                hf_copy(zs).start()

        lhs = hid[:, :, pl.ds(pl.multiple_of(p * kd, 128), kd)].reshape(th, kd)
        rhs = headt[pl.ds(2 * p, 2)].reshape(kd, cs)
        logits[...] += jnp.dot(lhs, rhs, preferred_element_type=jnp.float32)

    lane = lax.broadcasted_iota(jnp.int32, (tb, 128), 1)

    for k in range(H):
        lk = logits[k * tb : (k + 1) * tb, :]
        top = jnp.max(lk, axis=1, keepdims=True)
        total = jnp.sum(jnp.exp(lk - top), axis=1, keepdims=True)
        table = jnp.where(lane == 0, top, total).T
        stat[k : k + 1, :] = table[0:1, :]
        stat[H + k : H + k + 1, :] = table[1:2, :]
    stat[2 * H : 2 * H + 1, :] = masses[0:1, :]

    def exchange(stage, n, me, to):
        start, arrive = share(stat.at[...], stat_in.at[stage], s_st.at[stage], r_st.at[stage], n, me, to)
        start()
        arrive()
        blocks = [stat[...]] + [stat_in[stage, o] for o in range(1, n)]
        top = functools.reduce(jnp.maximum, [b[0:H] for b in blocks])
        total = functools.reduce(jnp.add, [b[H : 2 * H] * jnp.exp(b[0:H] - top) for b in blocks])
        stat[0:H, :] = top
        stat[H : 2 * H, :] = total

    exchange(0, X, x, to_x)
    exchange(1, Y, y, to_y)
    stat_in[2, 0] = stat[...]
    exchange(2, Z, z, lambda i: dev(x, y, c, i))

    for k in range(H):
        pltpu.make_async_copy(teach.at[k], teach.at[k], r_te.at[k]).wait()

    hops = ring_hops(Z, 2)
    nsub = dg.shape[2]
    tsub = th // nsub

    def dl_copy(direction, i):
        to = lax.rem(z + 1, Z) if direction == 0 else lax.rem(z + Z - 1, Z)
        return rc(
            delta.at[pl.ds(i * tsub, tsub)],
            dg.at[zl, c, i],
            s_dl.at[direction, i],
            r_dl.at[zl, c, i],
            dev(x, y, zh, to),
        )

    def dl_local(i):
        return rc(delta.at[pl.ds(i * tsub, tsub)], dg.at[zl, c, i], s_dl.at[2, i], r_dl.at[zl, c, i], partner)

    both_ways = min(hops[0] + hops[1]) > 0

    def send_delta(i):
        dl_copy(0, i).start()
        if both_ways:
            dl_copy(1, i).start()
        else:

            @pl.when(c == 1)
            def _():
                dl_copy(1, i).start()

        @pl.when(zh != c)
        def _():
            dl_local(i).start()

        @pl.when(zh == c)
        def _():
            pltpu.make_async_copy(delta.at[pl.ds(i * tsub, tsub)], dg.at[zl, c, i], r_dl.at[zl, c, i]).start()

    final = stat[...]
    lse = final[0:H] + jnp.log(final[H : 2 * H])
    mass = jnp.concatenate(
        [stat_in[2, lax.rem(c * H + k + Z - z, Z), 2 * H : 2 * H + 1, :] for k in range(H)], axis=0
    )
    scale = loss_scale / mass
    rows = jnp.concatenate([lse, scale, jnp.zeros((128 - 2 * H, 128), jnp.float32)], axis=0).T

    for k in range(H):
        lk = logits[k * tb : (k + 1) * tb, :]
        tk = teach[k].astype(jnp.float32)
        student = jnp.exp(lk - rows[:, k : k + 1])
        delta[k * tb : (k + 1) * tb, :] = (loss_scale * student - tk * rows[:, H + k : H + k + 1]).astype(
            jnp.bfloat16
        )
        if (k + 1) % (H // nsub) == 0:
            send_delta((k + 1) // (H // nsub) - 1)

    for k in range(H):
        lk = logits[k * tb : (k + 1) * tb, :]
        tk = teach[k].astype(jnp.float32)
        live = tk > 0.0
        term = jnp.where(live, tk * (jnp.log(jnp.where(live, tk, 1.0)) - lk), 0.0)
        table = jnp.broadcast_to(jnp.sum(term, axis=1, keepdims=True), (tb, 128)).T
        terms[k : k + 1, :] = table[0:1, :]
    term_x = share(terms.at[...], term_in.at[0], s_tm.at[0], r_tm.at[0], X, x, to_x)
    term_y = share(terms.at[...], term_in.at[1], s_tm.at[1], r_tm.at[1], Y, y, to_y)
    term_x[0]()

    def term_z(o):
        zd = lax.rem(z + o, Z)
        return zd, rc(terms.at[...], term_in.at[2, Z - o], s_tz.at[o], r_tm.at[2], dev(x, y, c, zd))

    def terms_to_y():
        term_x[1]()
        summed(terms, term_in.at[0], X)
        term_y[0]()

    def terms_to_z():
        term_y[1]()
        summed(terms, term_in.at[1], Y)
        for o in order:
            zd, copy = term_z(o)

            @pl.when(lax.div(zd, H) == c)
            def _():
                copy.start()

    def finish_terms():
        for o in order:
            zd, copy = term_z(o)

            @pl.when(lax.div(zd, H) == c)
            def _():
                copy.wait_send()

        @pl.when(zh == c)
        def _():
            all_in = term_in.at[2, pl.ds(1, Z - 1)]
            pltpu.make_async_copy(all_in, all_in, r_tm.at[2]).wait()
            total = terms[0:H, :]
            for o in range(1, Z):
                total = total + term_in[2, o, 0:H, :]
            kl = total / mass - jnp.log(mass) + lse
            pick = lax.broadcasted_iota(jnp.int32, (H, 128), 0) == zl
            fin[0:1, :] = jnp.sum(jnp.where(pick, lse, 0.0), axis=0, keepdims=True)
            fin[1:2, :] = jnp.sum(jnp.where(pick, kl, 0.0), axis=0, keepdims=True)
            fi_copy.start()

    fi_copy = rc(fin.at[...], fin_in.at[...], s_fi, r_fi, partner)

    head_copy.wait()
    gt[...] = jnp.zeros_like(gt)
    pltpu.make_async_copy(hidt.at[pc], hidt.at[pc], r_ht).wait()

    def to_gt(kk):
        cols = pl.ds(pl.multiple_of(kk * cs, cs), cs)
        for h in range(2):
            gt[h] += lax.dot_general(
                head[:, cols], dg[kk, h].reshape(th, cs), (((1,), (1,)), ((), ())), preferred_element_type=jnp.float32
            )

    def to_ghead(kk):
        cols = pl.ds(pl.multiple_of(kk * cs, cs), cs)
        res[...] = jnp.dot(hidt[0], dg[kk, 0].reshape(th, cs), preferred_element_type=jnp.float32) + jnp.dot(
            hidt[1], dg[kk, 1].reshape(th, cs), preferred_element_type=jnp.float32
        )
        ghead[:, cols] = res[pl.ds(pl.multiple_of(off, 64), db), :].astype(jnp.bfloat16)

    def ghead_copy(kk):
        cols = pl.ds(pl.multiple_of(kk * cs, cs), cs)
        return pltpu.make_async_copy(ghead.at[:, cols], ghead_out.at[:, cols], s_gh.at[kk])

    def dl_arrived(kk, part, i):
        pltpu.make_async_copy(dg.at[kk, part, i], dg.at[kk, part, i], r_dl.at[kk, part, i]).wait()

    def df_copy(kk, part, i, direction):
        to = lax.rem(z + 1, Z) if direction == 0 else lax.rem(z + Z - 1, Z)
        view = dg.at[kk, part, i]
        return rc(view, view, s_df.at[kk, part, i], r_dl.at[kk, part, i], dev(x, y, c, to))

    def hop_source(direction, s):
        return lax.rem(z - s + Z, Z) if direction == 0 else lax.rem(z + s, Z)

    for s in range(0, Z // 2 + 1):
        for i in range(nsub if s else 0):
            for part in range(2):
                for direction in range(2):
                    if s <= hops[part][direction]:
                        zs = hop_source(direction, s)
                        kk = lax.rem(zs, H)

                        @pl.when(lax.div(zs, H) == c)
                        def _():
                            dl_arrived(kk, part, i)
                            if s < hops[part][direction]:
                                df_copy(kk, part, i, direction).start()

        if s == 0:

            @pl.when(zh == c)
            def _():
                for part in range(2):
                    for i in range(nsub):
                        dl_arrived(zl, part, i)
                to_gt(zl)
        else:

            @pl.loop(0, 1 if 2 * s == Z else 2)
            def _(i):
                zs = lax.rem(z + Z - s + 2 * s * i, Z)

                @pl.when(lax.div(zs, H) == c)
                def _():
                    to_gt(lax.rem(zs, H))

        if s == 1:
            terms_to_y()
        if s == min(2, Z // 2):
            terms_to_z()

    nd = gx.shape[0]
    rows = db // nd
    sub = db // Y
    x_order = sorted(range(X), key=lambda o: -min(o, X - o))

    def gc_copy(dh, o):
        block = tokens_of(lax.rem(x + o, X), pc, z)
        lanes = pl.ds(pl.multiple_of(block * tb, tb), tb)
        return rc(
            gt.at[pc, pl.ds(dh * rows, rows), lanes], gc.at[dh, o], s_gc, r_gc.at[dh, o], partner
        )

    def gx_copy(dh, o):
        return rc(gsum.at[dh, o], gx.at[dh, X - o], s_gx, r_gx.at[dh], to_x(lax.rem(x + o, X)))

    for dh in range(nd):
        for o in x_order:
            gc_copy(dh, o).start()
    for dh in range(nd):
        for o in x_order:
            block = tokens_of(lax.rem(x + o, X), c, z)
            lanes = pl.ds(pl.multiple_of(block * tb, tb), tb)
            pltpu.make_async_copy(gc.at[dh, o], gc.at[dh, o], r_gc.at[dh, o]).wait()
            gsum[dh, o] = gt[c, dh * rows : (dh + 1) * rows, lanes] + gc[dh, o]
            if o:
                gx_copy(dh, o).start()

    @pl.loop(0, H)
    def _(kk):
        to_ghead(kk)
        ghead_copy(kk).start()

    finish_terms()

    def gy_copy(o):
        yd = lax.rem(y + o, Y)
        i = rows_of(yd, z)
        return i, rc(
            gx.at[lax.div(i * nd, Y), 0, pl.ds(pl.multiple_of(lax.rem(i, Y // nd) * sub, sub), sub), :],
            gy.at[Y - o],
            s_gy,
            r_gy,
            to_y(yd),
        )

    y_order = sorted(range(1, Y), key=lambda o: -min(o, Y - o))
    for dh in range(nd):
        acc = gsum[dh, 0]
        if X > 1:
            all_in = gx.at[dh, pl.ds(1, X - 1)]
            pltpu.make_async_copy(all_in, all_in, r_gx.at[dh]).wait()
        for o in range(1, X):
            acc = acc + gx[dh, o]
        gx[dh, 0] = acc
        for o in y_order:
            i, copy = gy_copy(o)

            @pl.when(lax.div(i * nd, Y) == dh)
            def _():
                copy.start()

    mine = rows_of(y, z)
    acc = gx[lax.div(mine * nd, Y), 0, pl.ds(pl.multiple_of(lax.rem(mine, Y // nd) * sub, sub), sub), :]
    if Y > 1:
        all_in = gy.at[pl.ds(1, Y - 1)]
        pltpu.make_async_copy(all_in, all_in, r_gy).wait()
    for o in range(1, Y):
        acc = acc + gy[o]
    gf[0] = acc

    go_copy = rc(gf.at[0], gf.at[1], s_go, r_go, {"vocab": vt, "tok": zt})
    go_local = pltpu.make_async_copy(gf.at[0], gf.at[1], r_go)

    @pl.when(at_home)
    def _():
        go_local.start()

    @pl.when(jnp.logical_not(at_home))
    def _():
        go_copy.start()

    @pl.when(zh == c)
    def _():
        fi_copy.wait_send()
        stat_out[...] = fin[...]

    @pl.when(zh != c)
    def _():
        pltpu.make_async_copy(fin_in.at[...], fin_in.at[...], r_fi).wait()
        stat_out[...] = fin_in[...]

    pltpu.make_async_copy(gc.at[...], gc.at[...], s_gc).wait()
    if X > 1:
        all_out = gx.at[:, pl.ds(1, X - 1)]
        pltpu.make_async_copy(all_out, all_out, s_gx).wait()
    if Y > 1:
        all_out = gy.at[pl.ds(1, Y - 1)]
        pltpu.make_async_copy(all_out, all_out, s_gy).wait()

    def drain(k0, kn, nrows, nlanes, sem):
        if min(kn, nrows, nlanes) > 0:
            view = hid.at[pl.ds(k0, kn), pl.ds(0, nrows), pl.ds(0, nlanes)]
            pltpu.make_async_copy(view, view, sem).wait()

    drain(0, split, pr, (X - 1) * plan, s_ga.at[0, 0])
    drain(0, split, (Y - 1) * pr, d, s_ga.at[0, 1])
    drain(split, H - split, (Y - 1) * pr, plan, s_ga.at[1, 0])
    drain(split, H - split, tb, (X - 1) * plan, s_ga.at[1, 1])
    for o in order:
        zd, copy = hz_copy(o)

        @pl.when(lax.div(zd, H) == c)
        def _():
            copy.wait_send()

        zd, copy = hd_copy(o)

        @pl.when(lax.div(zd, H) == c)
        def _():
            copy.wait_send()

        zd, copy = te_copy(o)

        @pl.when(lax.div(zd, H) == c)
        def _():
            copy.wait_send()

        zs = lax.rem(z + o, Z)

        @pl.when(lax.div(zs, H) == c)
        def _():
            hf_copy(zs).wait_send()

    @pl.when(zh == c)
    def _():
        own_head.wait_send()

    ht_copy.wait_send()
    for i in range(nsub):
        dl_copy(0, i).wait_send()
        if both_ways:
            dl_copy(1, i).wait_send()
        else:

            @pl.when(c == 1)
            def _():
                dl_copy(1, i).wait_send()

        @pl.when(zh != c)
        def _():
            dl_local(i).wait_send()

        for s in range(1, Z // 2 + 1):
            for part in range(2):
                for direction in range(2):
                    if s < hops[part][direction]:
                        zs = hop_source(direction, s)

                        @pl.when(lax.div(zs, H) == c)
                        def _():
                            df_copy(lax.rem(zs, H), part, i, direction).wait_send()

    @pl.when(jnp.logical_not(at_home))
    def _():
        go_copy.wait_send()

    for kk in range(H):
        ghead_copy(kk).wait()

    go_local.wait()
    ghid_out[...] = gf[1]


def per_device(geo, hidden, head, teacher, block_ids, counts):
    X, Y, Z, blk = geo
    H = Z // 2
    tb, d = hidden.shape
    db, cb = head.shape
    cs, th = cb // H, tb * H
    win = -(-db // 128) * 128
    sub = db // Y
    f32, bf16 = jnp.float32, jnp.bfloat16
    dma = pltpu.SemaphoreType.DMA
    most = max(X, Y)
    half = max(most // 2, 1)
    nd = 2 if Y % 2 == 0 else 1
    nsub = 2 if H % 2 == 0 else 1
    scratch = [
        pltpu.VMEM((db, cb), bf16),
        pltpu.VMEM((tb, cb), bf16),
        pltpu.VMEM((tb, cb), bf16),
        pltpu.VMEM((H, tb, d), bf16),
        pltpu.VMEM((Z, db, cs), bf16),
        pltpu.VMEM((H, tb, cs), bf16),
        pltpu.VMEM((th, cs), f32),
        pltpu.VMEM((8, 128), f32),
        pltpu.VMEM((3, max(X, Y), 8, 128), f32),
        pltpu.VMEM((8, 128), f32),
        pltpu.VMEM((3, max(X, Y, Z), 8, 128), f32),
        pltpu.VMEM((4 * H, 128), f32),
        pltpu.VMEM((3, max(X, Y, Z), 4 * H, 128), f32),
        pltpu.VMEM((th, cs), bf16),
        pltpu.VMEM((H, 2, nsub, th // nsub, cs), bf16),
        pltpu.VMEM((2, win, th), bf16),
        pltpu.VMEM((win, cs), f32),
        pltpu.VMEM((db, cb), bf16),
        pltpu.VMEM((2, db, th), f32),
        pltpu.VMEM((nd, X, db // nd, tb), f32),
        pltpu.VMEM((nd, X, db // nd, tb), f32),
        pltpu.VMEM((Y, sub, tb), f32),
        pltpu.VMEM((2, sub, tb), f32),
        pltpu.VMEM((nd, X, db // nd, tb), f32),
        pltpu.VMEM((8, 128), f32),
        pltpu.VMEM((8, 128), f32),
        dma((2,)), dma((H,)),
        dma((Z,)), dma((H,)),
        dma((2, 2)), dma((2, 2, half)), dma((2, max(X * Y, 2 * X, 2 * Y))),
        dma((Z,)), dma((H,)), dma((Z,)),
        dma((Z,)), dma((H,)),
        dma((3,)), dma((3,)),
        dma((2,)), dma((3,)), dma((Z,)),
        dma((3,)), dma((3,)),
        dma((3, nsub)), dma((H, 2, nsub)), dma((H, 2, nsub)),
        dma, dma,
        dma, dma((nd, X)),
        dma, dma((nd,)),
        dma, dma,
        dma, dma,
        dma, dma,
    ]
    vm = pl.BlockSpec(memory_space=pltpu.VMEM)
    hbm = pl.BlockSpec(memory_space=pl.ANY)
    sm = pl.BlockSpec(memory_space=pltpu.SMEM)
    ghead, ghid, stats = pl.pallas_call(
        functools.partial(kernel_body, geo),
        out_shape=(
            jax.ShapeDtypeStruct((db, cb), bf16),
            jax.ShapeDtypeStruct((sub, tb), f32),
            jax.ShapeDtypeStruct((8, 128), f32),
        ),
        in_specs=[hbm, hbm, hbm, sm, sm],
        out_specs=(hbm, vm, vm),
        scratch_shapes=scratch,
        compiler_params=pltpu.CompilerParams(has_side_effects=True, collective_id=0, vmem_limit_bytes=60 * 2**20),
    )(hidden, head, teacher, block_ids, counts)

    def place(
        stats_in, ghid_in, ghead_in, lse_to, kl_to, ghid_to, ghead_to, stats_at, ghid_at, ghead_at, in_sem, out_sem
    ):
        moves = [(stats_in, stats_at), (ghid_in, ghid_at)]
        parts = [pl.ds(k * cs, cs) for k in range(H)]
        moves += [(ghead_in.at[:, part], ghead_at.at[:, part]) for part in parts]
        loads = [pltpu.make_async_copy(src, dst, in_sem.at[k]) for k, (src, dst) in enumerate(moves)]
        for load in loads:
            load.start()
        loads[0].wait()
        stores = [
            pltpu.make_async_copy(stats_at.at[pl.ds(0, 1)], lse_to, out_sem.at[0]),
            pltpu.make_async_copy(stats_at.at[pl.ds(1, 1)], kl_to, out_sem.at[1]),
        ]
        stores[0].start()
        stores[1].start()
        loads[1].wait()
        stores.append(pltpu.make_async_copy(ghid_at, ghid_to, out_sem.at[2]))
        stores[2].start()
        for k, part in enumerate(parts):
            loads[2 + k].wait()
            stores.append(pltpu.make_async_copy(ghead_at.at[:, part], ghead_to.at[:, part], out_sem.at[3 + k]))
            stores[3 + k].start()
        for store in stores:
            store.wait()

    lse, kl, ghid, ghead = pl.pallas_call(
        place,
        out_shape=(
            jax.ShapeDtypeStruct((1, tb), f32),
            jax.ShapeDtypeStruct((1, tb), f32),
            jax.ShapeDtypeStruct(ghid.shape, f32),
            jax.ShapeDtypeStruct(ghead.shape, bf16),
        ),
        in_specs=[hbm, hbm, hbm],
        out_specs=(hbm, hbm, hbm, hbm),
        scratch_shapes=[
            pltpu.VMEM((8, 128), f32),
            pltpu.VMEM(ghid.shape, f32),
            pltpu.VMEM(ghead.shape, bf16),
            dma((2 + H,)),
            dma((3 + H,)),
        ],
    )(stats, ghid, ghead)
    return lse.reshape(tb), kl.reshape(tb), ghid.T, ghead


def solution(mesh, ring_y=RING_Y, blk=BLK):
    vocab, tok = mesh.shape["vocab"], mesh.shape["tok"]
    geo = (vocab // (2 * ring_y), ring_y, tok, blk)
    placed = (P("tok", None), P("tok", "vocab"), P("tok", "vocab"), P("tok", None), P("tok"))
    return jax.shard_map(
        functools.partial(per_device, geo),
        mesh=mesh,
        in_specs=placed,
        out_specs=(P("tok"), P("tok"), P("tok", "vocab"), P("tok", "vocab")),
        check_vma=False,
    )
```

time: 169 us -> 140 us (0.83)
  the two profiles are of different devices: /device:TPU:21 before, /device:TPU:62 now
where the time goes in v2:
time: 140 us
  Pallas kernels  139 us (99%)
    pallas_call x1, Pallas kernels, per_device(): pl.pallas_call(functools.partial(kernel_body, geo), out_shape=(jax.ShapeD...  137 us

profile of v2, /device:TPU:62, one launch (start us, length us, event | category | flops | bytes accessed | tf_op | source)
XLA Modules:
  0.0 140.1 jit_solution(14402984883184402064)
XLA Ops:
  1.3 136.6 %shard_map.84 = (bf16[448,1536]{1,0:T(8,128)(2,1)}, f32[56,128]{1,0:T(8,128)}, f32[8,128]{1,0:T(8,128)}) custom-call(bf16[128,3584]{1,0:T(8,128)(2,1)} %hidden.1, bf16[448,1536]{1,0:T(8,128)(2,1)} %head_in.1, bf16[128,1536]{1,0:T(8,128)(2,1)} %teacher_in.1, s32[1,16]{1,0:T(1,128)} %ids.1, s32[1]{0:T(128)S(6)} %copy.9.counts), custom_call_target="tpu_custom_call" | custom-call | tf_op jit(solution)/shard_map/pallas_call | solution.py:805
  137.9 2.2 %shard_map.85 = (f32[1,128]{1,0:T(1,128)}, f32[1,128]{1,0:T(1,128)}, f32[56,128]{1,0:T(8,128)}, bf16[448,1536]{1,0:T(8,128)(2,1)}) custom-call(f32[8,128]{1,0:T(8,128)} %get-tuple-element.11.stats_in, f32[56,128]{1,0:T(8,128)} %get-tuple-element.12.ghid_in, bf16[448,1536]{1,0:T(8,128)(2,1)} %get-tuple-element.13.ghead_in), custom_call_target="tpu_custom_call" | custom-call | tf_op jit(solution)/shard_map/pallas_call | solution.py:844

commit v3 on v2

--- a/solution.py
+++ b/solution.py
@@ -24,8 +24,8 @@
     geo,
     hidden, head_in, teacher_in, ids, counts,
     ghead_out, ghid_out, stat_out,
-    head, teacher, kept, hid, headt, teach, logits, masses, mass_in, terms, term_in, stat, stat_in, delta, dg, hidt, res, ghead, gt, gc, gx, gy, gf, gsum, fin, fin_in,
-    s_in, s_gh, s_hz, r_hz, s_ga, r_ga, r_gb, s_hd, s_hf, r_hd, s_te, r_te, s_ms, r_ms, s_tm, r_tm, s_tz, s_st, r_st, s_dl, s_df, r_dl, s_ht, r_ht,
+    head, teacher, kept, hid, headt, teach, logits, masses, mass_in, mass_of, terms, term_in, stat, stat_in, delta, dg, hidt, res, ghead, gt, gc, gx, gy, gf, gsum, fin, fin_in,
+    s_in, s_gh, s_hz, r_hz, s_ga, r_ga, r_gb, s_hd, s_hf, r_hd, s_te, r_te, s_ms, r_ms, s_mz, r_mz, s_tm, r_tm, s_tz, s_st, r_st, s_dl, s_df, r_dl, s_ht, r_ht,
     s_gc, r_gc, s_gx, r_gx, s_gy, r_gy, s_go, r_go, s_fi, r_fi,
 ):
     X, Y, Z, blk = geo
@@ -104,7 +104,7 @@
 
     def hz_copy(o):
         zd = lax.rem(z + o, Z)
-        return zd, rc(piece, piece_to, s_hz.at[o], r_hz.at[zl], dev(x, y, zh, zd))
+        return zd, rc(piece, piece_to, s_hz.at[lax.rem(zd, H)], r_hz.at[zl], dev(x, y, zh, zd))
 
     for o in order:
         zd, copy = hz_copy(o)
@@ -155,7 +155,7 @@
     def te_copy(o):
         zd = lax.rem(z + o, Z)
         cols = pl.ds(pl.multiple_of(lax.rem(zd, H) * cs, cs), cs)
-        return zd, rc(kept.at[:, cols], teach.at[zl], s_te.at[o], r_te.at[zl], dev(x, y, zh, zd))
+        return zd, rc(kept.at[:, cols], teach.at[zl], s_te.at[lax.rem(zd, H)], r_te.at[zl], dev(x, y, zh, zd))
 
     for o in order:
         zd, copy = te_copy(o)
@@ -203,10 +203,7 @@
     masses[...] = masses[...] + mass_in[0, 0]
     mass_x[0]()
 
-    for k in range(H):
-        pltpu.make_async_copy(piece, hid.at[k, pl.ds(row0, pr), pl.ds(lane0, plan)], r_hz.at[k]).wait()
-
-    def gather(g, first, second, block):
+    def gather(g, planes, first, second, block):
         (n1, me1, to1), (n2, me2, to2) = first, second
         hops1 = ring_hops(n1, 1)[0]
 
@@ -235,6 +232,9 @@
             source, device = along(n2, me2, direction, s, to2)
             view = block(lax.rem(me1 + q, n1), source)
             rc(view, view, s_ga.at[g, 1], r_gb.at[g, (2 * q + direction) * (n2 // 2) + s - 1], device).start()
+
+        for k in planes:
+            pltpu.make_async_copy(piece, hid.at[k, pl.ds(row0, pr), pl.ds(lane0, plan)], r_hz.at[k]).wait()
 
         progress = {}
 
@@ -300,36 +300,45 @@
     early = Z // 4
     split = H if H == 1 else H // 2
     x_first = gather(
-        0, (X, x, to_x), (Y, y, to_y), lambda i, j: hid.at[pl.ds(0, split), rows_at(j), lanes_at(i)]
+        0, range(split), (X, x, to_x), (Y, y, to_y), lambda i, j: hid.at[pl.ds(0, split), rows_at(j), lanes_at(i)]
     )
     y_first = gather(
-        1, (Y, y, to_y), (X, x, to_x), lambda i, j: hid.at[pl.ds(split, H - split), rows_at(i), lanes_at(j)]
+        1, range(split, H), (Y, y, to_y), (X, x, to_x), lambda i, j: hid.at[pl.ds(split, H - split), rows_at(i), lanes_at(j)]
     )
     todo = [x_first] if split == H else [x_first, y_first]
     turn = 0
     while todo:
         todo = [walk for walk in todo if next(walk, todo) is not todo]
         turn += 1
-        if turn == 3:
+        if turn == 8:
             mass_x[1]()
             summed(masses, mass_in.at[1], X)
             mass_y[0]()
-        if turn == 10 and early >= 1:
-            head_onward(1)
-            head_onward(Z - 1)
-    if turn < 3:
+    if turn < 8:
         mass_x[1]()
         summed(masses, mass_in.at[1], X)
         mass_y[0]()
-    if turn < 10 and early >= 1:
-        head_onward(1)
-        head_onward(Z - 1)
-    for o in range(2, early + 1):
+    for o in range(1, early + 1):
         head_onward(o)
         head_onward(Z - o)
 
     mass_y[1]()
     summed(masses, mass_in.at[2], Y)
+
+    def mass_z(o):
+        zd = lax.rem(z + o, Z)
+        return zd, rc(masses, mass_of.at[zl], s_mz.at[lax.rem(zd, H)], r_mz.at[zl], dev(x, y, zh, zd))
+
+    for o in order:
+        zd, copy = mass_z(o)
+
+        @pl.when(lax.div(zd, H) == c)
+        def _():
+            copy.start()
+
+    @pl.when(zh == c)
+    def _():
+        pltpu.make_async_copy(masses, mass_of.at[zl], r_mz.at[zl]).start()
 
     win = hidt.shape[1]
     win0 = lax.div(z * db, 128) * 128
@@ -371,7 +380,6 @@
         table = jnp.where(lane == 0, top, total).T
         stat[k : k + 1, :] = table[0:1, :]
         stat[H + k : H + k + 1, :] = table[1:2, :]
-    stat[2 * H : 2 * H + 1, :] = masses[0:1, :]
 
     def exchange(stage, n, me, to):
         start, arrive = share(stat.at[...], stat_in.at[stage], s_st.at[stage], r_st.at[stage], n, me, to)
@@ -385,7 +393,6 @@
 
     exchange(0, X, x, to_x)
     exchange(1, Y, y, to_y)
-    stat_in[2, 0] = stat[...]
     exchange(2, Z, z, lambda i: dev(x, y, c, i))
 
     for k in range(H):
@@ -430,9 +437,9 @@
 
     final = stat[...]
     lse = final[0:H] + jnp.log(final[H : 2 * H])
-    mass = jnp.concatenate(
-        [stat_in[2, lax.rem(c * H + k + Z - z, Z), 2 * H : 2 * H + 1, :] for k in range(H)], axis=0
-    )
+    for k in range(H):
+        pltpu.make_async_copy(mass_of.at[k], mass_of.at[k], r_mz.at[k]).wait()
+    mass = jnp.concatenate([mass_of[k, 0:1, :] for k in range(H)], axis=0)
     scale = loss_scale / mass
     rows = jnp.concatenate([lse, scale, jnp.zeros((128 - 2 * H, 128), jnp.float32)], axis=0).T
 
@@ -459,7 +466,7 @@
 
     def term_z(o):
         zd = lax.rem(z + o, Z)
-        return zd, rc(terms.at[...], term_in.at[2, Z - o], s_tz.at[o], r_tm.at[2], dev(x, y, c, zd))
+        return zd, rc(terms.at[...], term_in.at[2, Z - o], s_tz.at[lax.rem(zd, H)], r_tm.at[2], dev(x, y, c, zd))
 
     def terms_to_y():
         term_x[1]()
@@ -519,7 +526,7 @@
 
     def ghead_copy(kk):
         cols = pl.ds(pl.multiple_of(kk * cs, cs), cs)
-        return pltpu.make_async_copy(ghead.at[:, cols], ghead_out.at[:, cols], s_gh.at[kk])
+        return pltpu.make_async_copy(ghead.at[:, cols], ghead_out.at[:, cols], s_gh)
 
     def dl_arrived(kk, part, i):
         pltpu.make_async_copy(dg.at[kk, part, i], dg.at[kk, part, i], r_dl.at[kk, part, i]).wait()
@@ -696,6 +703,12 @@
         def _():
             copy.wait_send()
 
+        zd, copy = mass_z(o)
+
+        @pl.when(lax.div(zd, H) == c)
+        def _():
+            copy.wait_send()
+
         zs = lax.rem(z + o, Z)
 
         @pl.when(lax.div(zs, H) == c)
@@ -735,8 +748,7 @@
     def _():
         go_copy.wait_send()
 
-    for kk in range(H):
-        ghead_copy(kk).wait()
+    pltpu.make_async_copy(ghead, ghead_out, s_gh).wait()
 
     go_local.wait()
     ghid_out[...] = gf[1]
@@ -766,10 +778,11 @@
         pltpu.VMEM((th, cs), f32),
         pltpu.VMEM((8, 128), f32),
         pltpu.VMEM((3, max(X, Y), 8, 128), f32),
+        pltpu.VMEM((H, 8, 128), f32),
         pltpu.VMEM((8, 128), f32),
         pltpu.VMEM((3, max(X, Y, Z), 8, 128), f32),
-        pltpu.VMEM((4 * H, 128), f32),
-        pltpu.VMEM((3, max(X, Y, Z), 4 * H, 128), f32),
+        pltpu.VMEM((2 * H, 128), f32),
+        pltpu.VMEM((3, max(X, Y, Z), 2 * H, 128), f32),
         pltpu.VMEM((th, cs), bf16),
         pltpu.VMEM((H, 2, nsub, th // nsub, cs), bf16),
         pltpu.VMEM((2, win, th), bf16),
@@ -783,13 +796,14 @@
         pltpu.VMEM((nd, X, db // nd, tb), f32),
         pltpu.VMEM((8, 128), f32),
         pltpu.VMEM((8, 128), f32),
-        dma((2,)), dma((H,)),
-        dma((Z,)), dma((H,)),
+        dma((2,)), dma,
+        dma((H,)), dma((H,)),
         dma((2, 2)), dma((2, 2, half)), dma((2, max(X * Y, 2 * X, 2 * Y))),
         dma((Z,)), dma((H,)), dma((Z,)),
-        dma((Z,)), dma((H,)),
+        dma((H,)), dma((H,)),
         dma((3,)), dma((3,)),
-        dma((2,)), dma((3,)), dma((Z,)),
+        dma((H,)), dma((H,)),
+        dma((2,)), dma((3,)), dma((H,)),
         dma((3,)), dma((3,)),
         dma((3, nsub)), dma((H, 2, nsub)), dma((H, 2, nsub)),
         dma, dma,

time: 140 us -> 138 us (0.986)
  Pallas kernels: 139 us -> 136 us
    pallas_call x1, Pallas kernels: 137 us -> 134 us  [per_device(): pl.pallas_call(functools.partial(kernel_body, geo), out_shape=(jax.ShapeD...]
where the time goes in v3:
time: 138 us; the launch traced here: 137 us
  Pallas kernels  136 us (99%)
    pallas_call x1, Pallas kernels, per_device(): pl.pallas_call(functools.partial(kernel_body, geo), out_shape=(jax.ShapeD...  134 us

profile of v3, /device:TPU:62, one launch (start us, length us, event | category | flops | bytes accessed | tf_op | source)
XLA Modules:
  0.0 137.3 jit_solution(12195632670939950560)
XLA Ops:
  1.3 133.9 %shard_map.84 = (bf16[448,1536]{1,0:T(8,128)(2,1)}, f32[56,128]{1,0:T(8,128)}, f32[8,128]{1,0:T(8,128)}) custom-call(bf16[128,3584]{1,0:T(8,128)(2,1)} %hidden.1, bf16[448,1536]{1,0:T(8,128)(2,1)} %head_in.1, bf16[128,1536]{1,0:T(8,128)(2,1)} %teacher_in.1, s32[1,16]{1,0:T(1,128)} %ids.1, s32[1]{0:T(128)S(6)} %copy.9.counts), custom_call_target="tpu_custom_call" | custom-call | tf_op jit(solution)/shard_map/pallas_call | solution.py:819
  135.1 2.2 %shard_map.85 = (f32[1,128]{1,0:T(1,128)}, f32[1,128]{1,0:T(1,128)}, f32[56,128]{1,0:T(8,128)}, bf16[448,1536]{1,0:T(8,128)(2,1)}) custom-call(f32[8,128]{1,0:T(8,128)} %get-tuple-element.11.stats_in, f32[56,128]{1,0:T(8,128)} %get-tuple-element.12.ghid_in, bf16[448,1536]{1,0:T(8,128)(2,1)} %get-tuple-element.13.ghead_in), custom_call_target="tpu_custom_call" | custom-call | tf_op jit(solution)/shard_map/pallas_call | solution.py:858

commit v4 on v3

--- a/solution.py
+++ b/solution.py
@@ -767,7 +767,7 @@
     most = max(X, Y)
     half = max(most // 2, 1)
     nd = 2 if Y % 2 == 0 else 1
-    nsub = 2 if H % 2 == 0 else 1
+    nsub = 4 if H % 4 == 0 else 2 if H % 2 == 0 else 1
     scratch = [
         pltpu.VMEM((db, cb), bf16),
         pltpu.VMEM((tb, cb), bf16),

time: 138 us -> 139 us (level)
  Pallas kernels: 136 us -> 138 us
    pallas_call x1, Pallas kernels: 134 us -> 136 us  [per_device(): pl.pallas_call(functools.partial(kernel_body, geo), out_shape=(jax.ShapeD...]
where the time goes in v4:
time: 139 us
  Pallas kernels  138 us (99%)
    pallas_call x1, Pallas kernels, per_device(): pl.pallas_call(functools.partial(kernel_body, geo), out_shape=(jax.ShapeD...  136 us

profile of v4, /device:TPU:62, one launch (start us, length us, event | category | flops | bytes accessed | tf_op | source)
XLA Modules:
  0.0 139.3 jit_solution(2386002885021890342)
XLA Ops:
  1.3 135.8 %shard_map.84 = (bf16[448,1536]{1,0:T(8,128)(2,1)}, f32[56,128]{1,0:T(8,128)}, f32[8,128]{1,0:T(8,128)}) custom-call(bf16[128,3584]{1,0:T(8,128)(2,1)} %hidden.1, bf16[448,1536]{1,0:T(8,128)(2,1)} %head_in.1, bf16[128,1536]{1,0:T(8,128)(2,1)} %teacher_in.1, s32[1,16]{1,0:T(1,128)} %ids.1, s32[1]{0:T(128)S(6)} %copy.9.counts), custom_call_target="tpu_custom_call" | custom-call | tf_op jit(solution)/shard_map/pallas_call | solution.py:819
  137.1 2.2 %shard_map.85 = (f32[1,128]{1,0:T(1,128)}, f32[1,128]{1,0:T(1,128)}, f32[56,128]{1,0:T(8,128)}, bf16[448,1536]{1,0:T(8,128)(2,1)}) custom-call(f32[8,128]{1,0:T(8,128)} %get-tuple-element.11.stats_in, f32[56,128]{1,0:T(8,128)} %get-tuple-element.12.ghid_in, bf16[448,1536]{1,0:T(8,128)(2,1)} %get-tuple-element.13.ghead_in), custom_call_target="tpu_custom_call" | custom-call | tf_op jit(solution)/shard_map/pallas_call | solution.py:858
